TPU v7x, 32 devices: a whole 2x2x4 slice. The times are simulated.
32 devices in a mesh: cfg: 2 (over y), space: 8 (over z, x), tm: 2 (over core).
Axes of the slice: x: 2, y: 2, z: 4, core: 2. Of those that a mesh axis runs over, the one named last changes fastest.
Arguments:
- eigvecs: bfloat16 [4, 2, 3, 1536, 256], P(('cfg', 'tm'), None, None, 'space'), parts along dimension 0, may hold values from -6 to 6
- momenta: int32 [3, 3], replicated, may hold values from -2 to 2, as said below
- pair_list: int32 [8, 2], P('tm'), may hold values from 0 to 1
- panels: bfloat16 [16, 2, 1024, 1024], P(('cfg', 'tm'), None, 'space'), parts along dimension 0, may hold values from -6 to 6
Outputs:
- dressed: bfloat16 [16, 3, 2, 1024, 1024], P(('cfg', 'tm'), None, None, 'space'), parts along dimension 0
There are 2 independent parts, one for each index of `cfg`. A program takes and returns all parts, laid end to end along the dimension named above; an argument that names none is the same for every part. Nothing has to cross between parts.
Inputs may be any that keep to these rules, and one draw needn't show every extreme that they name: `momenta`: the first component of every momentum is nonzero.
All inputs are finite; a program needn't handle non-finite values.
Results may differ from a plain program's by a relative error of at most 0.0075.
Values may be sent and summed in bfloat16 or wider, within the bound.
A program may use at most 64 MiB of HBM per device.

v0:
```python
import math

import jax
import jax.numpy as jnp
from jax import lax
from jax.sharding import PartitionSpec as P

LX = 64


def phased_block(cosine, sine_part, real_part, imag_part):
    cos_col = cosine[:, None]
    sin_col = sine_part[:, None]
    wave_re = cos_col * real_part + sin_col * imag_part
    wave_im = cos_col * imag_part - sin_col * real_part
    upper = jnp.concatenate([wave_re, wave_im], -1)
    lower = jnp.concatenate([wave_im, -wave_re], -1)
    return jnp.stack([upper, lower], -4).astype(jnp.bfloat16)


def local(eigvecs, momenta, pair_list, panels):
    slice_count, _, colors, slab_sites, vectors = eigvecs.shape
    mom_count = momenta.shape[0]
    space_count = lax.axis_size("space")
    first_site = lax.axis_index("space") * slab_sites
    site_index = first_site + jnp.arange(slab_sites, dtype=jnp.int32)
    xpos = site_index % LX
    ypos = site_index // LX % LX
    zpos = site_index // (LX * LX)
    wave = (
        momenta[:, 0:1] * xpos[None, :]
        + momenta[:, 1:2] * ypos[None, :]
        + momenta[:, 2:3] * zpos[None, :]
    )
    wave = jnp.mod(wave, LX)
    angle = wave.astype(jnp.float32) * jnp.float32(2.0 * math.pi / LX)
    cosine = jnp.cos(angle)
    sine_part = jnp.sin(angle)
    factor = 1.0 / math.sqrt(6.0 * slab_sites * space_count * vectors)
    real_part = eigvecs[:, 0].astype(jnp.float32)
    imag_part = eigvecs[:, 1].astype(jnp.float32)
    phased_all = jnp.concatenate(
        [
            phased_block(cosine[moment], sine_part[moment], real_part, imag_part)
            for moment in range(mom_count)
        ],
        -1,
    )
    phased_all = phased_all.reshape(slice_count, 2, colors, slab_sites, mom_count, 2 * vectors)
    gram_local = jnp.einsum(
        "trcsk,trcsml->tmkl", eigvecs, phased_all, preferred_element_type=jnp.float32
    )
    gram_local = factor * gram_local
    summed = lax.psum(gram_local, "space")
    own_fields = summed.astype(jnp.bfloat16)
    meson_fields = lax.all_gather(own_fields, "tm", axis=0, tiled=True)
    pair_count = pair_list.shape[0]
    panel_rows = panels.shape[2]
    panel_width = panels.shape[3]
    spins = panel_width // vectors
    source_fields = jnp.take(meson_fields, pair_list[:, 0], axis=0).reshape(
        pair_count, mom_count, vectors, 2, vectors
    )
    sink_fields = jnp.take(meson_fields, pair_list[:, 1], axis=0).reshape(
        pair_count, mom_count, vectors, 2, vectors
    )
    panel_parts = panels.reshape(pair_count, 2, panel_rows, spins, vectors)
    panel_re = panel_parts[:, 0]
    panel_im = panel_parts[:, 1]
    panel_mix = jnp.stack(
        [jnp.stack([panel_re, panel_im], 1), jnp.stack([panel_im, -panel_re], 1)], 1
    )
    right_dressed = jnp.einsum(
        "porxbk,pmlrk->pmoxbl", panel_mix, source_fields, preferred_element_type=jnp.float32
    )
    right_dressed = right_dressed.astype(jnp.bfloat16).reshape(
        pair_count * mom_count, 2, panel_rows, panel_width
    )
    turned = lax.all_to_all(right_dressed, "space", split_axis=3, concat_axis=2, tiled=True)
    column_count = turned.shape[3]
    turned = turned.reshape(pair_count, mom_count, 2, spins, vectors, column_count)
    turned_re = turned[:, :, 0]
    turned_im = turned[:, :, 1]
    mixed_parts = jnp.stack(
        [jnp.stack([turned_re, -turned_im], 2), jnp.stack([turned_im, turned_re], 2)], 2
    )
    dressed = jnp.einsum(
        "pmorajc,pmkrj->pmocak", mixed_parts, sink_fields, preferred_element_type=jnp.float32
    )
    return dressed.reshape(pair_count, mom_count, 2, column_count, panel_width).astype(jnp.bfloat16)


def solution(mesh):
    placed = (
        P(("cfg", "tm"), None, None, "space", None),
        P(),
        P("tm", None),
        P(("cfg", "tm"), None, "space", None),
    )
    return jax.shard_map(
        local,
        mesh=mesh,
        in_specs=placed,
        out_specs=P(("cfg", "tm"), None, None, "space", None),
        check_vma=False,
    )
```

profile of v0, /device:TPU:0, one launch (start us, length us, event | category | flops | bytes accessed | tf_op | source)
XLA Modules:
  0.0 343.8 jit_solution(5193341892418195743)
XLA Ops:
  6.6 1.0 slice_reduce_fusion.2
  7.6 0.1 fusion.37
  7.8 1.6 fusion.30
  9.6 0.3 fusion.28
  10.1 1.2 fusion.17
  11.3 83.3 %all-reduce.1 = bf16[1,3,256,512]{2,3,1,0:T(8,128)(2,1)S(1)} all-reduce(f32[1,3,256,512]{2,3,1,0:T(8,128)S(1)} %fusion.17), channel_id=1, replica_groups=mesh['cfg'=2,'space'=8,'tm'=2] {'space'}, use_global_device_ids=true, to_apply=%region_0.1 | all-reduce | flops 393216 | bytes 2359296 | tf_op jit(solution)/shard_map/psum | solution.py:54
  94.7 1.3 copy.48
  95.9 3.0 copy.49
  99.0 1.5 fusion.42
  100.4 1.5 copy.77
  102.0 1.2 neg.44
  103.2 2.4 copy.76
  105.6 2.3 copy.53
  107.9 2.7 maximum_bitcast_fusion.6
  110.7 2.2 gather_fusion.1
  112.8 2.0 broadcast_select_fusion
  114.9 3.8 %reshape.415 = bf16[4,3,256,2,256]{4,3,2,1,0:T(2,128)(2,1)S(1)} reshape(bf16[4,3,256,512]{3,2,1,0:T(8,128)(2,1)} %broadcast_select_fusion) | data formatting | bytes 6291456 | tf_op jit(solution)/shard_map/reshape | solution.py:61
  118.6 6.2 %bitcast_convert_fusion.1 = bf16[4,3,256,2,128,4]{4,2,5,3,1,0:T(8,128)(2,1)S(1)} fusion(bf16[4,1,2,128,4,256]{5,3,2,4,1,0:T(8,128)(2,1)} %maximum_bitcast_fusion.6, bf16[4,1,2,128,4,256]{5,3,2,4,1,0:T(8,128)(2,1)} %copy.53, bf16[4,3,256,2,256,1,1]{4,3,2,1,0,6,5:T(2,128)(2,1)S(1)} %bitcast.120), kind=kOutput, calls=%fused_computation.7 | convolution fusion | flops 3232759808 | bytes 13631488 | tf_op jit(solution)/shard_map/porxbk,pmlrk->pmoxbl/dot_general | solution.py:73
  124.8 36.6 %copy.55 = bf16[12,2,128,1024]{2,1,0,3:T(2,128)(2,1)} copy(bf16[12,2,128,1024]{2,3,1,0:T(8,128)(2,1)S(1)} %bitcast.117) | data formatting | bytes 12582912 | tf_op jit(solution)/shard_map/reshape | solution.py:76
  161.5 5.1 %all-to-all-start = ((bf16[12,2,128,1024]{2,1,0,3:T(2,128)(2,1)}), bf16[12,2,128,1024]{2,1,0,3:T(2,128)(2,1)}, u32[]{:S(2)}, u32[]{:S(2)}) async-start(bf16[12,2,128,1024]{2,1,0,3:T(2,128)(2,1)} %copy.55), calls=%async_computation | async-start | bytes 12582912 | tf_op jit(solution)/shard_map/all_to_all | solution.py:79
  166.6 2.5 gather_fusion
  169.0 2.3 broadcast_select_fusion.1
  171.3 3.1 reshape.414
  174.3 125.2 %all-to-all-done = bf16[12,2,128,1024]{2,1,0,3:T(2,128)(2,1)} async-done(((bf16[12,2,128,1024]{2,1,0,3:T(2,128)(2,1)}), bf16[12,2,128,1024]{2,1,0,3:T(2,128)(2,1)}, u32[]{:S(2)}, u32[]{:S(2)}) %all-to-all-start) | async-done | bytes 6291488 | tf_op jit(solution)/shard_map/all_to_all | solution.py:79
  299.6 6.9 %copy.56 = bf16[12,2,128,1024]{2,3,1,0:T(8,128)(2,1)} copy(bf16[12,2,128,1024]{2,1,0,3:T(2,128)(2,1)} %all-to-all-done) | data formatting | bytes 12582912 | tf_op jit(solution)/shard_map/all_to_all | solution.py:79
  306.4 8.6 %copy.57 = bf16[12,2,8,128,128]{4,3,2,1,0:T(8,128)(2,1)} copy(bf16[12,2,8,128,128]{3,4,2,1,0:T(8,128)(2,1)} %bitcast.114) | data formatting | bytes 12582912 | tf_op jit(solution)/shard_map/all_to_all | solution.py:79
  315.1 3.4 slice_bitcast_fusion
  318.5 1.2 copy-done
  319.7 0.4 fusion.41
  320.1 1.0 maximum_bitcast_fusion
  321.1 7.2 %bitcast_convert_fusion = bf16[4,3,256,2,4,128]{5,2,4,3,1,0:T(8,128)(2,1)} fusion(bf16[4,3,1,2,4,256,128]{6,5,3,4,2,1,0:T(8,128)(2,1)S(1)} %get-tuple-element.16, bf16[4,3,1,2,4,256,128]{6,5,3,4,2,1,0:T(8,128)(2,1)S(1)} %get-tuple-element.15, bf16[4,3,256,2,256,1,1]{4,3,2,1,0,6,5:T(2,128)(2,1)} %bitcast.119), kind=kOutput, calls=%fused_computation.6 | convolution fusion | flops 3249537024 | bytes 22020096 | tf_op jit(solution)/shard_map/pmorajc,pmkrj->pmocak/dot_general | solution.py:87
  328.3 8.6 %copy.62 = bf16[4,3,2,128,1024]{4,3,2,1,0:T(8,128)(2,1)} copy(bf16[4,3,2,128,1024]{3,4,2,1,0:T(8,128)(2,1)} %bitcast.118) | data formatting | bytes 12582912 | tf_op jit(solution)/shard_map/convert_element_type | solution.py:90
  (22 shorter events, 0.5 us)
Async XLA Ops:
  6.5 104.1 %all-gather.2.cloned.1.call-start = ((), (), s32[]{:S(2)}) async-start(), calls=%async_computation.1 | async-start | bytes 2359296 | tf_op jit(solution)/shard_map/all_gather | solution.py:56
  7.7 1.8 copy-start.3
  103.2 4.7 %copy-start.4 = (s32[4,2]{0,1:T(2,128)S(1)}, s32[4,2]{0,1:T(2,128)}, u32[]{:S(2)}) copy-start(s32[4,2]{0,1:T(2,128)} %param.8) | copy-start | bytes 100
  103.2 4.7 %copy-start.2 = (bf16[4,1,128,4,256]{4,2,1,3,0:T(8,128)(2,1)S(1)}, bf16[4,1,128,4,256]{4,2,1,3,0:T(8,128)(2,1)}, u32[]{:S(2)}) copy-start(bf16[4,1,128,4,256]{4,2,1,3,0:T(8,128)(2,1)} %neg.44) | copy-start | bytes 3145732
  161.5 5.1 %copy-start.1 = (bf16[2,3,256,512]{3,2,1,0:T(8,128)(2,1)S(1)}, bf16[2,3,256,512]{3,2,1,0:T(8,128)(2,1)}, u32[]{:S(2)}) copy-start(bf16[2,3,256,512]{3,2,1,0:T(8,128)(2,1)} %all-gather.2.cloned.1.call-done) | copy-start | bytes 4718596
  161.5 138.1 %all-to-all-start = ((bf16[12,2,128,1024]{2,1,0,3:T(2,128)(2,1)}), bf16[12,2,128,1024]{2,1,0,3:T(2,128)(2,1)}, u32[]{:S(2)}, u32[]{:S(2)}) async-start(bf16[12,2,128,1024]{2,1,0,3:T(2,128)(2,1)} %copy.55), calls=%async_computation | async-start | bytes 12582912 | tf_op jit(solution)/shard_map/all_to_all | solution.py:79
  315.1 4.6 %copy-start = (bf16[12,2,8,128,128]{4,3,2,1,0:T(8,128)(2,1)S(1)}, bf16[12,2,8,128,128]{4,3,2,1,0:T(8,128)(2,1)}, u32[]{:S(2)}) copy-start(bf16[12,2,8,128,128]{4,3,2,1,0:T(8,128)(2,1)} %copy.57) | copy-start | bytes 18874372
Sparse Core Ops, SparseCore 0:
  96.1 7.9 all-gather.1
where the time goes:
time: 345 us; the launch traced here: 344 us
  waiting for transfers between devices  125 us (36%)
  local copies, waits for them, and re-layouts  89.8 us (26%)
  blocking collectives  83.3 us (24%)
  matrix products  14.6 us (4%)
  between operations  13.6 us (4%)
  other arithmetic  12 us (3%)
  starting transfers between devices  5.08 us (1%)
    all_to_all x1, waiting for transfers between devices, local(): lax.all_to_all(right_dressed, 'space', split_axis=3, concat_axis=2, tiled...  125 us
    psum x1, blocking collectives, local(): summed = lax.psum(gram_local, 'space')  83.3 us
    reshape x1, local copies, waits for them, and re-layouts, local(): right_dressed.astype(jnp.bfloat16)  36.6 us
    all_to_all x2, local copies, waits for them, and re-layouts, local(): lax.all_to_all(right_dressed, 'space', split_axis=3, concat_axis=2, tiled...  15.5 us
    unnamed x14, local copies, waits for them, and re-layouts  11.6 us
    convert_element_type x1, local copies, waits for them, and re-layouts, local(): dressed.reshape(pair_count, mom_count, 2, column_count, panel_width)  8.62 us
    dot_general x1, matrix products, local(): jnp.einsum('pmorajc,pmkrj->pmocak', mixed_parts, sink_fields, preferred_e...  7.2 us
  transfers between devices with their start and end apart: 2, of which 1 were waited for; matrix products, arithmetic and copies ran while one was open for 7% of the time, Pallas kernels for 0%

commit v1 on v0

--- a/solution.py
+++ b/solution.py
@@ -1,11 +1,379 @@
+import functools
 import math
 
 import jax
 import jax.numpy as jnp
 from jax import lax
+from jax.experimental import pallas as pl
+from jax.experimental.pallas import tpu as pltpu
 from jax.sharding import PartitionSpec as P
 
 LX = 64
+MESH = pl.DeviceIdType.MESH
+
+
+def phase_table(momenta, first_site, slab_sites):
+    site_index = first_site + jnp.arange(slab_sites, dtype=jnp.int32)
+    xpos = site_index % LX
+    ypos = site_index // LX % LX
+    zpos = site_index // (LX * LX)
+    wave = (
+        momenta[:, 0:1] * xpos[None, :]
+        + momenta[:, 1:2] * ypos[None, :]
+        + momenta[:, 2:3] * zpos[None, :]
+    )
+    wave = jnp.mod(wave, LX)
+    angle = wave.astype(jnp.float32) * jnp.float32(2.0 * math.pi / LX)
+    return jnp.cos(angle), jnp.sin(angle)
+
+
+def exchange_kernel(
+    factor, blocks, eig, trig, pan, tau, mes,
+    stack, wave, gram, part, got_half, half32, half16, got_piece,
+    s_half, r_half, s_piece, r_piece, s_field, r_field, s_swap, r_swap,
+    s_core, r_core, s_pan, r_pan, s_own, r_own, s_fwd, r_fwd, s_loc,
+):
+    space = lax.axis_index("space")
+    core = lax.axis_index("tm")
+    block = space // 2
+    side = space % 2
+    other_side = block * 2 + (1 - side)
+    pairs, _, rows, _ = pan.shape
+    moms, vectors, _ = gram.shape
+    colors, sites = eig.shape[2], eig.shape[3]
+    hrows = vectors // 2
+    prows = hrows // blocks
+
+    def peer(step):
+        return lax.rem(block + step, blocks)
+
+    def sender(step):
+        return lax.rem(block + blocks - step, blocks)
+
+    def at(index):
+        return {"space": index}
+
+    barrier = pltpu.get_barrier_semaphore()
+    for step in range(1, blocks):
+        pl.semaphore_signal(
+            barrier, inc=1, device_id=at(peer(step) * 2 + side), device_id_type=MESH
+        )
+    pl.semaphore_signal(barrier, inc=1, device_id=at(other_side), device_id_type=MESH)
+    pl.semaphore_signal(barrier, inc=1, device_id={"tm": 1 - core}, device_id_type=MESH)
+    pl.semaphore_wait(barrier, blocks + 1)
+
+    def remote(src, dst, send, recv, device):
+        return pltpu.make_async_remote_copy(
+            src_ref=src, dst_ref=dst, send_sem=send, recv_sem=recv,
+            device_id=device, device_id_type=MESH,
+        )
+
+    def tau_rows(owner):
+        return pl.ds(pl.multiple_of(owner * rows, rows), rows)
+
+    def pan_cols(index):
+        return pl.ds(pl.multiple_of(index * vectors, vectors), vectors)
+
+    along = [
+        [
+            remote(
+                pan.at[p, :, :, pan_cols(peer(step))], tau.at[p, :, tau_rows(space), :],
+                s_pan.at[p, step - 1], r_pan.at[p, step - 1], at(peer(step) * 2 + side),
+            )
+            for step in range(1, blocks)
+        ]
+        for p in range(pairs)
+    ]
+    own = [
+        remote(
+            pan.at[p, :, :, pan_cols(block)], tau.at[p, :, tau_rows(space), :],
+            s_own.at[p], r_own.at[p], at(other_side),
+        )
+        for p in range(pairs)
+    ]
+    keep = [
+        pltpu.make_async_copy(
+            pan.at[p, :, :, pan_cols(block)], tau.at[p, :, tau_rows(space), :], s_loc.at[p]
+        )
+        for p in range(pairs)
+    ]
+    forward = [
+        [
+            remote(
+                tau.at[p, :, tau_rows(sender(step) * 2 + side), :],
+                tau.at[p, :, tau_rows(sender(step) * 2 + side), :],
+                s_fwd.at[p, step - 1], r_fwd.at[p, step - 1], at(other_side),
+            )
+            for step in range(1, blocks)
+        ]
+        for p in range(pairs)
+    ]
+    my_half = pl.ds(pl.multiple_of(side * hrows, hrows), hrows)
+    far_half = pl.ds(pl.multiple_of((1 - side) * hrows, hrows), hrows)
+    my_piece = pl.ds(pl.multiple_of(side * hrows + block * prows, prows), prows)
+    halves = [
+        remote(part.at[m, far_half, :], got_half.at[m], s_half.at[m], r_half.at[m], at(other_side))
+        for m in range(moms)
+    ]
+    pieces = [
+        [
+            remote(
+                half16.at[m, pl.ds(pl.multiple_of(peer(step) * prows, prows), prows), :],
+                got_piece.at[step - 1, m],
+                s_piece.at[m, step - 1], r_piece.at[m, step - 1], at(peer(step) * 2 + side),
+            )
+            for step in range(1, blocks)
+        ]
+        for m in range(moms)
+    ]
+    fields = [
+        [
+            remote(
+                mes.at[core, m, my_piece, :], mes.at[core, m, my_piece, :],
+                s_field.at[m, step - 1], r_field.at[m, step - 1], at(peer(step) * 2 + side),
+            )
+            for step in range(1, blocks)
+        ]
+        for m in range(moms)
+    ]
+    swaps = [
+        remote(
+            mes.at[core, m, my_half, :], mes.at[core, m, my_half, :],
+            s_swap.at[m], r_swap.at[m], at(other_side),
+        )
+        for m in range(moms)
+    ]
+    cores = [
+        [
+            remote(
+                mes.at[core, m, which, :], mes.at[core, m, which, :],
+                s_core.at[m, i], r_core.at[m, i], {"tm": 1 - core},
+            )
+            for i, which in enumerate((my_half, far_half))
+        ]
+        for m in range(moms)
+    ]
+
+    def send_along(p):
+        for copy in along[p]:
+            copy.start()
+
+    def pass_on(p):
+        for step in range(blocks - 1):
+            along[p][step].wait_recv()
+            forward[p][step].start()
+
+    send_along(0)
+    own[0].start()
+    for copy in keep:
+        copy.start()
+
+    for color in range(colors):
+        for r in range(2):
+            stack[pl.ds((r * colors + color) * sites, sites), :] = eig[0, r, color]
+    for m in range(moms):
+        cos_col = trig[:, m : m + 1]
+        sin_col = trig[:, moms + m : moms + m + 1]
+        for color in range(colors):
+            real_part = eig[0, 0, color].astype(jnp.float32)
+            imag_part = eig[0, 1, color].astype(jnp.float32)
+            wave_re = (cos_col * real_part + sin_col * imag_part).astype(jnp.bfloat16)
+            wave_im = (cos_col * imag_part - sin_col * real_part).astype(jnp.bfloat16)
+            upper = pl.ds(color * sites, sites)
+            lower = pl.ds((colors + color) * sites, sites)
+            wave[upper, :vectors] = wave_re
+            wave[upper, vectors:] = wave_im
+            wave[lower, :vectors] = wave_im
+            wave[lower, vectors:] = -wave_re
+        total = factor * lax.dot_general(
+            stack[...], wave[...], (((0,), (0,)), ((), ())), preferred_element_type=jnp.float32
+        )
+        gram[m] = total
+        part[m] = total.astype(jnp.bfloat16)
+        halves[m].start()
+
+    for m in range(moms):
+        halves[m].wait_recv()
+        value = gram[m, my_half, :] + got_half[m].astype(jnp.float32)
+        half32[m] = value
+        half16[m] = value.astype(jnp.bfloat16)
+        for copy in pieces[m]:
+            copy.start()
+    if pairs > 1:
+        send_along(1)
+    for p in range(1, pairs):
+        own[p].start()
+    pass_on(0)
+
+    for m in range(moms):
+        value = half32[m, pl.ds(pl.multiple_of(block * prows, prows), prows), :]
+        for step in range(blocks - 1):
+            pieces[m][step].wait_recv()
+            value = value + got_piece[step, m].astype(jnp.float32)
+        mes[core, m, my_piece, :] = value.astype(jnp.bfloat16)
+        for copy in fields[m]:
+            copy.start()
+    for p in range(2, pairs):
+        send_along(p)
+    if pairs > 1:
+        pass_on(1)
+    for m in range(moms):
+        for copy in fields[m]:
+            copy.wait_recv()
+        swaps[m].start()
+        cores[m][0].start()
+    if pairs > 2:
+        pass_on(2)
+    for m in range(moms):
+        swaps[m].wait_recv()
+        cores[m][1].start()
+    for p in range(3, pairs):
+        pass_on(p)
+
+    for m in range(moms):
+        halves[m].wait_send()
+        swaps[m].wait_send()
+        for copy in pieces[m] + fields[m]:
+            copy.wait_send()
+        for copy in cores[m]:
+            copy.wait()
+    for p in range(pairs):
+        keep[p].wait()
+        own[p].wait()
+        for copy in along[p]:
+            copy.wait_send()
+        for copy in forward[p]:
+            copy.wait()
+
+
+def exchange(eigvecs, trig, panels, spins):
+    pairs, _, rows, width = panels.shape
+    _, _, colors, sites, vectors = eigvecs.shape
+    moms = trig.shape[1] // 2
+    space_count = lax.axis_size("space")
+    slices = lax.axis_size("tm")
+    factor = 1.0 / math.sqrt(6.0 * sites * space_count * vectors)
+    hrows = vectors // 2
+    prows = hrows // spins
+    bf16, f32 = jnp.bfloat16, jnp.float32
+    dma = pltpu.SemaphoreType.DMA
+    others = spins - 1
+    vmem = pl.BlockSpec(memory_space=pltpu.VMEM)
+    return pl.pallas_call(
+        functools.partial(exchange_kernel, factor, spins),
+        out_shape=(
+            jax.ShapeDtypeStruct((pairs, 2, rows * space_count, vectors), bf16),
+            jax.ShapeDtypeStruct((slices, moms, vectors, 2 * vectors), bf16),
+        ),
+        in_specs=[vmem] * 3,
+        out_specs=(pl.BlockSpec(memory_space=pl.ANY), vmem),
+        scratch_shapes=[
+            pltpu.VMEM((2 * colors * sites, vectors), bf16),
+            pltpu.VMEM((2 * colors * sites, 2 * vectors), bf16),
+            pltpu.VMEM((moms, vectors, 2 * vectors), f32),
+            pltpu.VMEM((moms, vectors, 2 * vectors), bf16),
+            pltpu.VMEM((moms, hrows, 2 * vectors), bf16),
+            pltpu.VMEM((moms, hrows, 2 * vectors), f32),
+            pltpu.VMEM((moms, hrows, 2 * vectors), bf16),
+            pltpu.VMEM((others, moms, prows, 2 * vectors), bf16),
+            dma((moms,)), dma((moms,)),
+            dma((moms, others)), dma((moms, others)),
+            dma((moms, others)), dma((moms, others)),
+            dma((moms,)), dma((moms,)),
+            dma((moms, 2)), dma((moms, 2)),
+            dma((pairs, others)), dma((pairs, others)),
+            dma((pairs,)), dma((pairs,)),
+            dma((pairs, others)), dma((pairs, others)),
+            dma((pairs,)),
+        ],
+        compiler_params=pltpu.CompilerParams(
+            collective_id=0, has_side_effects=True, vmem_limit_bytes=40 << 20
+        ),
+        name="exchange",
+    )(eigvecs, trig, panels)
+
+
+def multiply_kernel(spins, list_ref, side_ref, tau, mes, out, left, right, sink):
+    pair = pl.program_id(0)
+    source = list_ref[pair, 0]
+    target = list_ref[pair, 1]
+    moms, vectors = mes.shape[1], mes.shape[2]
+    cols = out.shape[3]
+    own = pl.ds(pl.multiple_of(side_ref[0] * cols, cols), cols)
+    for m in range(moms):
+        real_part = mes[source, m, own, :vectors]
+        imag_part = mes[source, m, own, vectors:]
+        left[pl.ds(2 * m * cols, cols), :vectors] = real_part
+        left[pl.ds(2 * m * cols, cols), vectors:] = imag_part
+        left[pl.ds((2 * m + 1) * cols, cols), :vectors] = -imag_part
+        left[pl.ds((2 * m + 1) * cols, cols), vectors:] = real_part
+    turned = (((1,), (1,)), ((), ()))
+    for spin in range(spins):
+        rows = pl.ds(spin * vectors, vectors)
+        value = lax.dot_general(
+            left[:, :vectors], tau[0, 0, rows, :], turned, preferred_element_type=jnp.float32
+        ) + lax.dot_general(
+            left[:, vectors:], tau[0, 1, rows, :], turned, preferred_element_type=jnp.float32
+        )
+        value = value.astype(jnp.bfloat16)
+        for m in range(moms):
+            for o in range(2):
+                right[m, pl.ds(spin * cols, cols), o * vectors : (o + 1) * vectors] = value[
+                    (2 * m + o) * cols : (2 * m + o + 1) * cols
+                ]
+    for m in range(moms):
+        real_part = mes[target, m, :, :vectors]
+        imag_part = mes[target, m, :, vectors:]
+        sink[:vectors, :vectors] = real_part
+        sink[:vectors, vectors:] = -imag_part
+        sink[vectors:, :vectors] = imag_part
+        sink[vectors:, vectors:] = real_part
+        value = lax.dot_general(
+            right[m], sink[...], turned, preferred_element_type=jnp.float32
+        ).astype(jnp.bfloat16)
+        for spin in range(spins):
+            for o in range(2):
+                out[0, m, o, :, pl.ds(spin * vectors, vectors)] = value[
+                    spin * cols : (spin + 1) * cols, o * vectors : (o + 1) * vectors
+                ]
+
+
+def multiply(pair_list, side, tau, mes, spins):
+    pairs, _, width, vectors = tau.shape
+    slices, moms = mes.shape[:2]
+    cols = width // lax.axis_size("space")
+    bf16 = jnp.bfloat16
+    return pl.pallas_call(
+        functools.partial(multiply_kernel, spins),
+        out_shape=jax.ShapeDtypeStruct((pairs, moms, 2, cols, width), bf16),
+        grid_spec=pltpu.PrefetchScalarGridSpec(
+            num_scalar_prefetch=2,
+            grid=(pairs,),
+            in_specs=[
+                pl.BlockSpec((1, 2, width, vectors), lambda p, *_: (p, 0, 0, 0)),
+                pl.BlockSpec(mes.shape, lambda p, *_: (0, 0, 0, 0)),
+            ],
+            out_specs=pl.BlockSpec((1, moms, 2, cols, width), lambda p, *_: (p, 0, 0, 0, 0)),
+            scratch_shapes=[
+                pltpu.VMEM((2 * moms * cols, 2 * vectors), bf16),
+                pltpu.VMEM((moms, spins * cols, 2 * vectors), bf16),
+                pltpu.VMEM((2 * vectors, 2 * vectors), bf16),
+            ],
+        ),
+        compiler_params=pltpu.CompilerParams(vmem_limit_bytes=40 << 20),
+        name="multiply",
+    )(pair_list, side, tau, mes)
+
+
+def local_kernels(eigvecs, momenta, pair_list, panels):
+    slab_sites, vectors = eigvecs.shape[3:]
+    spins = panels.shape[3] // vectors
+    space = lax.axis_index("space")
+    cosine, sine = phase_table(momenta, space * slab_sites, slab_sites)
+    trig = jnp.concatenate([cosine, sine], 0).T
+    tau, mes = exchange(eigvecs, trig, panels, spins)
+    side = jnp.reshape(space % 2, (1,)).astype(jnp.int32)
+    return multiply(pair_list, side, tau, mes, spins)
 
 
 def phased_block(cosine, sine_part, real_part, imag_part):
@@ -18,24 +386,11 @@
     return jnp.stack([upper, lower], -4).astype(jnp.bfloat16)
 
 
-def local(eigvecs, momenta, pair_list, panels):
+def local_general(eigvecs, momenta, pair_list, panels):
     slice_count, _, colors, slab_sites, vectors = eigvecs.shape
     mom_count = momenta.shape[0]
     space_count = lax.axis_size("space")
-    first_site = lax.axis_index("space") * slab_sites
-    site_index = first_site + jnp.arange(slab_sites, dtype=jnp.int32)
-    xpos = site_index % LX
-    ypos = site_index // LX % LX
-    zpos = site_index // (LX * LX)
-    wave = (
-        momenta[:, 0:1] * xpos[None, :]
-        + momenta[:, 1:2] * ypos[None, :]
-        + momenta[:, 2:3] * zpos[None, :]
-    )
-    wave = jnp.mod(wave, LX)
-    angle = wave.astype(jnp.float32) * jnp.float32(2.0 * math.pi / LX)
-    cosine = jnp.cos(angle)
-    sine_part = jnp.sin(angle)
+    cosine, sine_part = phase_table(momenta, lax.axis_index("space") * slab_sites, slab_sites)
     factor = 1.0 / math.sqrt(6.0 * slab_sites * space_count * vectors)
     real_part = eigvecs[:, 0].astype(jnp.float32)
     imag_part = eigvecs[:, 1].astype(jnp.float32)
@@ -90,6 +445,21 @@
     return dressed.reshape(pair_count, mom_count, 2, column_count, panel_width).astype(jnp.bfloat16)
 
 
+def local(eigvecs, momenta, pair_list, panels):
+    slices, _, _, _, vectors = eigvecs.shape
+    spins = panels.shape[3] // vectors
+    fits = (
+        slices == 1
+        and lax.axis_size("tm") == 2
+        and lax.axis_size("space") == 2 * spins
+        and spins > 1
+        and panels.shape[2] * 2 == vectors
+        and panels.shape[2] % 128 == 0
+        and (vectors // 2) % (16 * spins) == 0
+    )
+    return (local_kernels if fits else local_general)(eigvecs, momenta, pair_list, panels)
+
+
 def solution(mesh):
     placed = (
         P(("cfg", "tm"), None, None, "space", None),

time: 345 us -> 95.3 us (0.28)
  waiting for transfers between devices: 125 us -> 0 us
  Pallas kernels: 0 us -> 90.3 us
  local copies, waits for them, and re-layouts: 89.8 us -> 4.54 us
  blocking collectives: 83.3 us -> 0 us
  matrix products: 14.6 us -> 0 us
  between operations: 13.6 us -> 0.04 us
  other arithmetic: 12 us -> 0.17 us
  starting transfers between devices: 5.08 us -> 0 us
    all_to_all x1 -> x0, waiting for transfers between devices: 125 us -> none  [local(): lax.all_to_all(right_dressed, 'space', split_axis=3, concat_axis=2, tiled...]
    pallas_call x0 -> x2, Pallas kernels: none -> 90.3 us  [the longest x1 81.2 us: exchange(): pl.pallas_call(functools.partial(exchange_kernel, factor, spins), out_sha...]
    psum x1 -> x0, blocking collectives: 83.3 us -> none  [local(): summed = lax.psum(gram_local, 'space')]
    reshape x3 -> x0, local copies, waits for them, and re-layouts: 43.4 us -> none  [the longest x1 36.6 us: local(): right_dressed.astype(jnp.bfloat16)]
    all_to_all x2 -> x0, local copies, waits for them, and re-layouts: 15.5 us -> none  [local(): lax.all_to_all(right_dressed, 'space', split_axis=3, concat_axis=2, tiled...]
    dot_general x3 -> x0, matrix products: 14.6 us -> none  [the longest x1 7.2 us: local(): jnp.einsum('pmorajc,pmkrj->pmocak', mixed_parts, sink_fields, preferred_e...]
    convert_element_type x2 -> x0, local copies, waits for them, and re-layouts: 9.89 us -> none  [the longest x1 8.62 us: local(): dressed.reshape(pair_count, mom_count, 2, column_count, panel_width)]
    unnamed x14 -> x5, local copies, waits for them, and re-layouts: 11.6 us -> 3.42 us
  transfers between devices with their start and end apart: 2 -> 0, of which waited for: 1 -> 0; matrix products, arithmetic and copies ran while one was open for 7% -> 0% of each run, Pallas kernels for 0% -> 0%
where the time goes in v1:
time: 95.3 us; the launch traced here: 95.1 us
  Pallas kernels  90.3 us (95%)
  local copies, waits for them, and re-layouts  4.54 us (5%)
    pallas_call x1, Pallas kernels, exchange(): pl.pallas_call(functools.partial(exchange_kernel, factor, spins), out_sha...  81.2 us
    pallas_call x1, Pallas kernels, multiply(): pl.pallas_call(functools.partial(multiply_kernel, spins), out_shape=jax.S...  9.11 us
    unnamed x5, local copies, waits for them, and re-layouts  3.42 us

profile of v1, /device:TPU:0, one launch (start us, length us, event | category | flops | bytes accessed | tf_op | source)
XLA Modules:
  0.0 95.1 jit_solution(11400895153542847065)
XLA Ops:
  0.0 1.0 %slice_reduce_fusion.2 = (s32[3]{0:T(128)S(1)}, s32[3]{0:T(128)S(1)}, s32[3]{0:T(128)S(1)}) fusion(s32[3,3]{1,0:T(4,128)} %param.5), kind=kLoop, calls=%fused_computation.11 | loop fusion | bytes 72 | tf_op jit(solution)/shard_map/slice | solution.py:21
  1.0 0.8 copy.7.list_ref
  1.8 0.1 fusion.6
  2.0 0.1 copy.6
  2.1 0.0 copy-start
  2.1 1.6 %copy-done = bf16[4,2,128,1024]{3,2,1,0:T(8,128)(2,1)S(1)} copy-done((bf16[4,2,128,1024]{3,2,1,0:T(8,128)(2,1)S(1)}, bf16[4,2,128,1024]{3,2,1,0:T(8,128)(2,1)}, u32[]{:S(2)}) %copy-start) | copy-done | bytes 2097176
  3.7 0.0 copy-start.1
  3.7 1.1 %copy-done.1 = bf16[1,2,3,192,256]{4,3,2,1,0:T(8,128)(2,1)S(1)} copy-done((bf16[1,2,3,192,256]{4,3,2,1,0:T(8,128)(2,1)S(1)}, bf16[1,2,3,192,256]{4,3,2,1,0:T(8,128)(2,1)}, u32[]{:S(2)}) %copy-start.1) | copy-done | bytes 589848
  4.7 81.2 %exchange.1 = (bf16[4,2,1024,256]{3,2,1,0:T(8,128)(2,1)S(1)}, bf16[2,3,256,512]{3,2,1,0:T(8,128)(2,1)S(1)}) custom-call(bf16[1,2,3,192,256]{4,3,2,1,0:T(8,128)(2,1)S(1)} %copy-done.1, f32[192,6]{1,0:T(8,128)S(1)} %bitcast.2, bf16[4,2,128,1024]{3,2,1,0:T(8,128)(2,1)S(1)} %copy-done), custom_call_target="tpu_custom_call" | custom-call | tf_op jit(solution)/shard_map/exchange/pallas_call | solution.py:262
  86.0 9.1 %multiply.1 = bf16[4,3,2,128,1024]{4,3,2,1,0:T(8,128)(2,1)} custom-call(s32[4,2]{1,0:T(4,128)S(1)} %copy.7.list_ref, s32[1]{0:T(128)} %bitcast.side_ref, bf16[4,2,1024,256]{3,2,1,0:T(8,128)(2,1)S(1)} %get-tuple-element.7.tau, bf16[2,3,256,512]{3,2,1,0:T(8,128)(2,1)S(1)} %get-tuple-element.8.mes), custom_call_target="tpu_custom_call" | custom-call | tf_op jit(solution)/shard_map/multiply/pallas_call | solution.py:346
  (3 shorter events, 0.0 us)
Async XLA Ops:
  2.1 1.6 %copy-start = (bf16[4,2,128,1024]{3,2,1,0:T(8,128)(2,1)S(1)}, bf16[4,2,128,1024]{3,2,1,0:T(8,128)(2,1)}, u32[]{:S(2)}) copy-start(bf16[4,2,128,1024]{3,2,1,0:T(8,128)(2,1)} %pan.1) | copy-start | bytes 6291460
  3.7 1.1 %copy-start.1 = (bf16[1,2,3,192,256]{4,3,2,1,0:T(8,128)(2,1)S(1)}, bf16[1,2,3,192,256]{4,3,2,1,0:T(8,128)(2,1)}, u32[]{:S(2)}) copy-start(bf16[1,2,3,192,256]{4,3,2,1,0:T(8,128)(2,1)} %eig.1) | copy-start | bytes 1769476

commit v2 on v1

--- a/solution.py
+++ b/solution.py
@@ -28,10 +28,10 @@
 
 
 def exchange_kernel(
-    factor, blocks, eig, trig, pan, tau, mes,
-    stack, wave, gram, part, got_half, half32, half16, got_piece,
+    factor, blocks, momenta, pair_list, eig_hbm, pan, out,
+    tau, mes, left, right, sink, made, eig, stack, wave, gram, part, got_half, half32, half16, got_piece,
     s_half, r_half, s_piece, r_piece, s_field, r_field, s_swap, r_swap,
-    s_core, r_core, s_pan, r_pan, s_own, r_own, s_fwd, r_fwd, s_loc,
+    s_core, r_core, s_pan, r_pan, s_own, r_own, s_fwd, r_fwd, s_loc, s_eig, s_out,
 ):
     space = lax.axis_index("space")
     core = lax.axis_index("tm")
@@ -40,15 +40,22 @@
     other_side = block * 2 + (1 - side)
     pairs, _, rows, _ = pan.shape
     moms, vectors, _ = gram.shape
-    colors, sites = eig.shape[2], eig.shape[3]
+    colors, sites = eig.shape[1], eig.shape[2]
     hrows = vectors // 2
     prows = hrows // blocks
 
+    fetch = pltpu.make_async_copy(eig_hbm.at[0], eig, s_eig)
+    fetch.start()
+
     def peer(step):
-        return lax.rem(block + step, blocks)
-
-    def sender(step):
-        return lax.rem(block + blocks - step, blocks)
+        index, bit = block, 1
+        while bit < blocks:
+            if (blocks - step) & bit:
+                index = index + bit * (1 - 2 * ((block // bit) % 2))
+            bit *= 2
+        return index
+
+    sender = peer
 
     def at(index):
         return {"space": index}
@@ -163,20 +170,89 @@
             along[p][step].wait_recv()
             forward[p][step].start()
 
-    send_along(0)
+    put = [pltpu.make_async_copy(made.at[p], out.at[p], s_out.at[p]) for p in range(pairs)]
+    turned = (((1,), (1,)), ((), ()))
+
+    def dress(p):
+        from_first = pair_list[0, p] == 0
+        to_first = pair_list[1, p] == 0
+        for m in range(moms):
+            field = jnp.where(from_first, mes[0, m, my_half, :], mes[1, m, my_half, :])
+            real_part = field[:, :vectors]
+            imag_part = field[:, vectors:]
+            left[pl.ds(2 * m * hrows, hrows), :vectors] = real_part
+            left[pl.ds(2 * m * hrows, hrows), vectors:] = imag_part
+            left[pl.ds((2 * m + 1) * hrows, hrows), :vectors] = -imag_part
+            left[pl.ds((2 * m + 1) * hrows, hrows), vectors:] = real_part
+        for spin in range(blocks):
+            spin_rows = pl.ds(spin * vectors, vectors)
+            value = lax.dot_general(
+                left[:, :vectors], tau[p, 0, spin_rows, :], turned,
+                preferred_element_type=jnp.float32,
+            ) + lax.dot_general(
+                left[:, vectors:], tau[p, 1, spin_rows, :], turned,
+                preferred_element_type=jnp.float32,
+            )
+            value = value.astype(jnp.bfloat16)
+            for m in range(moms):
+                for o in range(2):
+                    right[m, pl.ds(spin * hrows, hrows), o * vectors : (o + 1) * vectors] = value[
+                        (2 * m + o) * hrows : (2 * m + o + 1) * hrows
+                    ]
+        for m in range(moms):
+            field = jnp.where(to_first, mes[0, m], mes[1, m])
+            real_part = field[:, :vectors]
+            imag_part = field[:, vectors:]
+            sink[:vectors, :vectors] = real_part
+            sink[:vectors, vectors:] = -imag_part
+            sink[vectors:, :vectors] = imag_part
+            sink[vectors:, vectors:] = real_part
+            value = lax.dot_general(
+                right[m], sink[...], turned, preferred_element_type=jnp.float32
+            ).astype(jnp.bfloat16)
+            for spin in range(blocks):
+                for o in range(2):
+                    made[p, m, o, :, pl.ds(spin * vectors, vectors)] = value[
+                        spin * hrows : (spin + 1) * hrows, o * vectors : (o + 1) * vectors
+                    ]
+        put[p].start()
+
+    def settle(p):
+        keep[p].wait()
+        own[p].wait_recv()
+        for copy in forward[p]:
+            copy.wait_recv()
+
+    for p in range(min(2, pairs)):
+        send_along(p)
     own[0].start()
     for copy in keep:
         copy.start()
 
+    site = space * sites + lax.broadcasted_iota(jnp.int32, (sites, 128), 0)
+    lane = lax.broadcasted_iota(jnp.int32, (sites, 128), 1)
+    turn = jnp.zeros((sites, 128), jnp.int32)
+    shift = LX.bit_length() - 1
+    for m in range(moms):
+        sum_m = (
+            momenta[m, 0] * (site & (LX - 1))
+            + momenta[m, 1] * (lax.shift_right_logical(site, shift) & (LX - 1))
+            + momenta[m, 2] * lax.shift_right_logical(site, 2 * shift)
+        )
+        turn = jnp.where(lane == m, sum_m & (LX - 1), turn)
+    angle = turn.astype(jnp.float32) * jnp.float32(2.0 * math.pi / LX)
+    cosine = jnp.cos(angle)
+    sine = jnp.sin(angle)
+    fetch.wait()
     for color in range(colors):
         for r in range(2):
-            stack[pl.ds((r * colors + color) * sites, sites), :] = eig[0, r, color]
-    for m in range(moms):
-        cos_col = trig[:, m : m + 1]
-        sin_col = trig[:, moms + m : moms + m + 1]
+            stack[pl.ds((r * colors + color) * sites, sites), :] = eig[r, color]
+    for m in range(moms):
+        cos_col = cosine[:, m : m + 1]
+        sin_col = sine[:, m : m + 1]
         for color in range(colors):
-            real_part = eig[0, 0, color].astype(jnp.float32)
-            imag_part = eig[0, 1, color].astype(jnp.float32)
+            real_part = eig[0, color].astype(jnp.float32)
+            imag_part = eig[1, color].astype(jnp.float32)
             wave_re = (cos_col * real_part + sin_col * imag_part).astype(jnp.bfloat16)
             wave_im = (cos_col * imag_part - sin_col * real_part).astype(jnp.bfloat16)
             upper = pl.ds(color * sites, sites)
@@ -192,6 +268,8 @@
         part[m] = total.astype(jnp.bfloat16)
         halves[m].start()
 
+    for p in range(1, pairs):
+        own[p].start()
     for m in range(moms):
         halves[m].wait_recv()
         value = gram[m, my_half, :] + got_half[m].astype(jnp.float32)
@@ -199,10 +277,8 @@
         half16[m] = value.astype(jnp.bfloat16)
         for copy in pieces[m]:
             copy.start()
-    if pairs > 1:
-        send_along(1)
-    for p in range(1, pairs):
-        own[p].start()
+    for p in range(2, min(3, pairs)):
+        send_along(p)
     pass_on(0)
 
     for m in range(moms):
@@ -213,7 +289,7 @@
         mes[core, m, my_piece, :] = value.astype(jnp.bfloat16)
         for copy in fields[m]:
             copy.start()
-    for p in range(2, pairs):
+    for p in range(3, pairs):
         send_along(p)
     if pairs > 1:
         pass_on(1)
@@ -227,29 +303,33 @@
     for m in range(moms):
         swaps[m].wait_recv()
         cores[m][1].start()
+    for m in range(moms):
+        for copy in cores[m]:
+            copy.wait_recv()
+    settle(0)
+    dress(0)
     for p in range(3, pairs):
         pass_on(p)
+    for p in range(1, pairs):
+        settle(p)
+        dress(p)
 
     for m in range(moms):
         halves[m].wait_send()
         swaps[m].wait_send()
-        for copy in pieces[m] + fields[m]:
+        for copy in pieces[m] + fields[m] + cores[m]:
             copy.wait_send()
-        for copy in cores[m]:
-            copy.wait()
     for p in range(pairs):
-        keep[p].wait()
-        own[p].wait()
-        for copy in along[p]:
+        own[p].wait_send()
+        for copy in along[p] + forward[p]:
             copy.wait_send()
-        for copy in forward[p]:
-            copy.wait()
-
-
-def exchange(eigvecs, trig, panels, spins):
+        put[p].wait()
+
+
+def exchange(eigvecs, momenta, pair_list, panels, spins):
     pairs, _, rows, width = panels.shape
     _, _, colors, sites, vectors = eigvecs.shape
-    moms = trig.shape[1] // 2
+    moms = momenta.shape[0]
     space_count = lax.axis_size("space")
     slices = lax.axis_size("tm")
     factor = 1.0 / math.sqrt(6.0 * sites * space_count * vectors)
@@ -258,16 +338,21 @@
     bf16, f32 = jnp.bfloat16, jnp.float32
     dma = pltpu.SemaphoreType.DMA
     others = spins - 1
-    vmem = pl.BlockSpec(memory_space=pltpu.VMEM)
+    smem = pl.BlockSpec(memory_space=pltpu.SMEM)
+    hbm = pl.BlockSpec(memory_space=pl.ANY)
     return pl.pallas_call(
         functools.partial(exchange_kernel, factor, spins),
-        out_shape=(
-            jax.ShapeDtypeStruct((pairs, 2, rows * space_count, vectors), bf16),
-            jax.ShapeDtypeStruct((slices, moms, vectors, 2 * vectors), bf16),
-        ),
-        in_specs=[vmem] * 3,
-        out_specs=(pl.BlockSpec(memory_space=pl.ANY), vmem),
+        out_shape=jax.ShapeDtypeStruct((pairs, moms, 2, rows, width), bf16),
+        in_specs=[smem, smem, hbm, hbm],
+        out_specs=hbm,
         scratch_shapes=[
+            pltpu.VMEM((pairs, 2, rows * space_count, vectors), bf16),
+            pltpu.VMEM((slices, moms, vectors, 2 * vectors), bf16),
+            pltpu.VMEM((2 * moms * hrows, 2 * vectors), bf16),
+            pltpu.VMEM((moms, spins * hrows, 2 * vectors), bf16),
+            pltpu.VMEM((2 * vectors, 2 * vectors), bf16),
+            pltpu.VMEM((pairs, moms, 2, rows, width), bf16),
+            pltpu.VMEM((2, colors, sites, vectors), bf16),
             pltpu.VMEM((2 * colors * sites, vectors), bf16),
             pltpu.VMEM((2 * colors * sites, 2 * vectors), bf16),
             pltpu.VMEM((moms, vectors, 2 * vectors), f32),
@@ -285,95 +370,19 @@
             dma((pairs,)), dma((pairs,)),
             dma((pairs, others)), dma((pairs, others)),
             dma((pairs,)),
+            dma,
+            dma((pairs,)),
         ],
         compiler_params=pltpu.CompilerParams(
-            collective_id=0, has_side_effects=True, vmem_limit_bytes=40 << 20
+            collective_id=0, has_side_effects=True, vmem_limit_bytes=60 << 20
         ),
         name="exchange",
-    )(eigvecs, trig, panels)
-
-
-def multiply_kernel(spins, list_ref, side_ref, tau, mes, out, left, right, sink):
-    pair = pl.program_id(0)
-    source = list_ref[pair, 0]
-    target = list_ref[pair, 1]
-    moms, vectors = mes.shape[1], mes.shape[2]
-    cols = out.shape[3]
-    own = pl.ds(pl.multiple_of(side_ref[0] * cols, cols), cols)
-    for m in range(moms):
-        real_part = mes[source, m, own, :vectors]
-        imag_part = mes[source, m, own, vectors:]
-        left[pl.ds(2 * m * cols, cols), :vectors] = real_part
-        left[pl.ds(2 * m * cols, cols), vectors:] = imag_part
-        left[pl.ds((2 * m + 1) * cols, cols), :vectors] = -imag_part
-        left[pl.ds((2 * m + 1) * cols, cols), vectors:] = real_part
-    turned = (((1,), (1,)), ((), ()))
-    for spin in range(spins):
-        rows = pl.ds(spin * vectors, vectors)
-        value = lax.dot_general(
-            left[:, :vectors], tau[0, 0, rows, :], turned, preferred_element_type=jnp.float32
-        ) + lax.dot_general(
-            left[:, vectors:], tau[0, 1, rows, :], turned, preferred_element_type=jnp.float32
-        )
-        value = value.astype(jnp.bfloat16)
-        for m in range(moms):
-            for o in range(2):
-                right[m, pl.ds(spin * cols, cols), o * vectors : (o + 1) * vectors] = value[
-                    (2 * m + o) * cols : (2 * m + o + 1) * cols
-                ]
-    for m in range(moms):
-        real_part = mes[target, m, :, :vectors]
-        imag_part = mes[target, m, :, vectors:]
-        sink[:vectors, :vectors] = real_part
-        sink[:vectors, vectors:] = -imag_part
-        sink[vectors:, :vectors] = imag_part
-        sink[vectors:, vectors:] = real_part
-        value = lax.dot_general(
-            right[m], sink[...], turned, preferred_element_type=jnp.float32
-        ).astype(jnp.bfloat16)
-        for spin in range(spins):
-            for o in range(2):
-                out[0, m, o, :, pl.ds(spin * vectors, vectors)] = value[
-                    spin * cols : (spin + 1) * cols, o * vectors : (o + 1) * vectors
-                ]
-
-
-def multiply(pair_list, side, tau, mes, spins):
-    pairs, _, width, vectors = tau.shape
-    slices, moms = mes.shape[:2]
-    cols = width // lax.axis_size("space")
-    bf16 = jnp.bfloat16
-    return pl.pallas_call(
-        functools.partial(multiply_kernel, spins),
-        out_shape=jax.ShapeDtypeStruct((pairs, moms, 2, cols, width), bf16),
-        grid_spec=pltpu.PrefetchScalarGridSpec(
-            num_scalar_prefetch=2,
-            grid=(pairs,),
-            in_specs=[
-                pl.BlockSpec((1, 2, width, vectors), lambda p, *_: (p, 0, 0, 0)),
-                pl.BlockSpec(mes.shape, lambda p, *_: (0, 0, 0, 0)),
-            ],
-            out_specs=pl.BlockSpec((1, moms, 2, cols, width), lambda p, *_: (p, 0, 0, 0, 0)),
-            scratch_shapes=[
-                pltpu.VMEM((2 * moms * cols, 2 * vectors), bf16),
-                pltpu.VMEM((moms, spins * cols, 2 * vectors), bf16),
-                pltpu.VMEM((2 * vectors, 2 * vectors), bf16),
-            ],
-        ),
-        compiler_params=pltpu.CompilerParams(vmem_limit_bytes=40 << 20),
-        name="multiply",
-    )(pair_list, side, tau, mes)
+    )(momenta, pair_list, eigvecs, panels)
 
 
 def local_kernels(eigvecs, momenta, pair_list, panels):
-    slab_sites, vectors = eigvecs.shape[3:]
-    spins = panels.shape[3] // vectors
-    space = lax.axis_index("space")
-    cosine, sine = phase_table(momenta, space * slab_sites, slab_sites)
-    trig = jnp.concatenate([cosine, sine], 0).T
-    tau, mes = exchange(eigvecs, trig, panels, spins)
-    side = jnp.reshape(space % 2, (1,)).astype(jnp.int32)
-    return multiply(pair_list, side, tau, mes, spins)
+    spins = panels.shape[3] // eigvecs.shape[4]
+    return exchange(eigvecs, momenta, pair_list.T, panels, spins)
 
 
 def phased_block(cosine, sine_part, real_part, imag_part):
@@ -453,6 +462,9 @@
         and lax.axis_size("tm") == 2
         and lax.axis_size("space") == 2 * spins
         and spins > 1
+        and spins & (spins - 1) == 0
+        and LX & (LX - 1) == 0
+        and momenta.shape[0] <= 128
         and panels.shape[2] * 2 == vectors
         and panels.shape[2] % 128 == 0
         and (vectors // 2) % (16 * spins) == 0

time: 95.3 us -> 98.3 us (1.031)
  local copies, waits for them, and re-layouts: 4.54 us -> 6.57 us
  Pallas kernels: 90.3 us -> 91.5 us
    pallas_call x1, Pallas kernels: 81.2 us -> 91.5 us  [exchange(): pl.pallas_call(functools.partial(exchange_kernel, factor, spins), out_sha...]
    pallas_call x1 -> x0, Pallas kernels: 9.11 us -> none  [multiply(): pl.pallas_call(functools.partial(multiply_kernel, spins), out_shape=jax.S...]
    unnamed x5 -> x1, local copies, waits for them, and re-layouts: 3.42 us -> 6.57 us
    slice x1 -> x0, local copies, waits for them, and re-layouts: 1.01 us -> none  [phase_table(): momenta[:, 0:1] * xpos[None, :] + momenta[:, 1:2] * ypos[None, :]]
where the time goes in v2:
time: 98.3 us; the launch traced here: 98.1 us
  Pallas kernels  91.5 us (93%)
  local copies, waits for them, and re-layouts  6.57 us (7%)
    pallas_call x1, Pallas kernels, exchange(): pl.pallas_call(functools.partial(exchange_kernel, factor, spins), out_sha...  91.5 us
    unnamed x1, local copies, waits for them, and re-layouts  6.57 us

profile of v2, /device:TPU:0, one launch (start us, length us, event | category | flops | bytes accessed | tf_op | source)
XLA Modules:
  0.0 98.1 jit_solution(751457951832358092)
XLA Ops:
  0.0 91.5 %exchange.1 = bf16[4,3,2,128,1024]{4,3,2,1,0:T(8,128)(2,1)} custom-call(s32[3,3]{1,0:T(4,128)} %momenta.1, s32[2,4]{1,0:T(2,128)} %bitcast.1, bf16[1,2,3,192,256]{4,3,2,1,0:T(8,128)(2,1)} %eig_hbm.1, bf16[4,2,128,1024]{3,2,1,0:T(8,128)(2,1)} %pan.1), custom_call_target="tpu_custom_call" | custom-call | tf_op jit(solution)/shard_map/exchange/pallas_call | solution.py:343
  91.5 6.6 %copy.6 = bf16[4,3,2,128,1024]{4,3,2,1,0:T(8,128)(2,1)} copy(bf16[4,3,2,128,1024]{4,3,2,1,0:T(8,128)(2,1)} %exchange.1) | data formatting | bytes 12582912

commit v3 on v2

--- a/solution.py
+++ b/solution.py
@@ -27,11 +27,95 @@
     return jnp.cos(angle), jnp.sin(angle)
 
 
+def products(from_first, to_first, half, tau, mes, made, left, right, sink):
+    moms, vectors = mes.shape[1], mes.shape[2]
+    spins = tau.shape[1] // vectors
+    cols = vectors // 2
+    turned = (((1,), (1,)), ((), ()))
+    for m in range(moms):
+        field = jnp.where(from_first, mes[0, m, half, :], mes[1, m, half, :])
+        real_part = field[:, :vectors]
+        imag_part = field[:, vectors:]
+        left[pl.ds(2 * m * cols, cols), :vectors] = real_part
+        left[pl.ds(2 * m * cols, cols), vectors:] = imag_part
+        left[pl.ds((2 * m + 1) * cols, cols), :vectors] = -imag_part
+        left[pl.ds((2 * m + 1) * cols, cols), vectors:] = real_part
+    for spin in range(spins):
+        rows = pl.ds(spin * vectors, vectors)
+        value = lax.dot_general(
+            left[:, :vectors], tau[0, rows, :], turned, preferred_element_type=jnp.float32
+        ) + lax.dot_general(
+            left[:, vectors:], tau[1, rows, :], turned, preferred_element_type=jnp.float32
+        )
+        value = value.astype(jnp.bfloat16)
+        for m in range(moms):
+            for o in range(2):
+                right[m, pl.ds(spin * cols, cols), o * vectors : (o + 1) * vectors] = value[
+                    (2 * m + o) * cols : (2 * m + o + 1) * cols
+                ]
+    for m in range(moms):
+        field = jnp.where(to_first, mes[0, m], mes[1, m])
+        real_part = field[:, :vectors]
+        imag_part = field[:, vectors:]
+        sink[:vectors, :vectors] = real_part
+        sink[:vectors, vectors:] = -imag_part
+        sink[vectors:, :vectors] = imag_part
+        sink[vectors:, vectors:] = real_part
+        value = lax.dot_general(
+            right[m], sink[...], turned, preferred_element_type=jnp.float32
+        ).astype(jnp.bfloat16)
+        for spin in range(spins):
+            for o in range(2):
+                made[m, o, :, pl.ds(spin * vectors, vectors)] = value[
+                    spin * cols : (spin + 1) * cols, o * vectors : (o + 1) * vectors
+                ]
+
+
+def finish_kernel(pair_list, side, done, tau, mes, out, made, left, right, sink, s_done, s_made):
+    last = out.shape[0] - 1
+    cols = mes.shape[2] // 2
+    copy = pltpu.make_async_copy(done, out.at[pl.ds(0, last)], s_done)
+    copy.start()
+    products(
+        pair_list[0, last] == 0, pair_list[1, last] == 0,
+        pl.ds(pl.multiple_of(side[0] * cols, cols), cols), tau, mes, made, left, right, sink,
+    )
+    ending = pltpu.make_async_copy(made, out.at[last], s_made)
+    ending.start()
+    copy.wait()
+    ending.wait()
+
+
+def finish(pair_list, side, done, tau, mes):
+    last, moms, _, cols, width = done.shape
+    vectors = mes.shape[2]
+    bf16 = jnp.bfloat16
+    smem = pl.BlockSpec(memory_space=pltpu.SMEM)
+    vmem = pl.BlockSpec(memory_space=pltpu.VMEM)
+    hbm = pl.BlockSpec(memory_space=pl.ANY)
+    return pl.pallas_call(
+        finish_kernel,
+        out_shape=jax.ShapeDtypeStruct((last + 1,) + done.shape[1:], bf16),
+        in_specs=[smem, smem, hbm, vmem, vmem],
+        out_specs=hbm,
+        scratch_shapes=[
+            pltpu.VMEM((moms, 2, cols, width), bf16),
+            pltpu.VMEM((2 * moms * cols, 2 * vectors), bf16),
+            pltpu.VMEM((moms, width // vectors * cols, 2 * vectors), bf16),
+            pltpu.VMEM((2 * vectors, 2 * vectors), bf16),
+            pltpu.SemaphoreType.DMA,
+            pltpu.SemaphoreType.DMA,
+        ],
+        compiler_params=pltpu.CompilerParams(vmem_limit_bytes=16 << 20),
+        name="finish",
+    )(pair_list, side, done, tau, mes)
+
+
 def exchange_kernel(
-    factor, blocks, momenta, pair_list, eig_hbm, pan, out,
-    tau, mes, left, right, sink, made, eig, stack, wave, gram, part, got_half, half32, half16, got_piece,
-    s_half, r_half, s_piece, r_piece, s_field, r_field, s_swap, r_swap,
-    s_core, r_core, s_pan, r_pan, s_own, r_own, s_fwd, r_fwd, s_loc, s_eig, s_out,
+    factor, blocks, momenta, pair_list, eig_hbm, pan, out, tau_last, mes_out,
+    tau, mes, left, right, sink, made, eig, stack, wave, gram, part, got,
+    s_sum, r_sum, s_field, r_field,
+    s_core, r_core, s_pan, r_pan, s_own, r_own, s_fwd, r_fwd, s_loc, s_eig, s_out, s_mes,
 ):
     space = lax.axis_index("space")
     core = lax.axis_index("tm")
@@ -42,7 +126,6 @@
     moms, vectors, _ = gram.shape
     colors, sites = eig.shape[1], eig.shape[2]
     hrows = vectors // 2
-    prows = hrows // blocks
 
     fetch = pltpu.make_async_copy(eig_hbm.at[0], eig, s_eig)
     fetch.start()
@@ -75,8 +158,9 @@
             device_id=device, device_id_type=MESH,
         )
 
-    def tau_rows(owner):
-        return pl.ds(pl.multiple_of(owner * rows, rows), rows)
+    def tau_rows(p, owner):
+        whole = tau_last if p == pairs - 1 else tau.at[p]
+        return whole.at[:, pl.ds(pl.multiple_of(owner * rows, rows), rows), :]
 
     def pan_cols(index):
         return pl.ds(pl.multiple_of(index * vectors, vectors), vectors)
@@ -84,7 +168,7 @@
     along = [
         [
             remote(
-                pan.at[p, :, :, pan_cols(peer(step))], tau.at[p, :, tau_rows(space), :],
+                pan.at[p, :, :, pan_cols(peer(step))], tau_rows(p, space),
                 s_pan.at[p, step - 1], r_pan.at[p, step - 1], at(peer(step) * 2 + side),
             )
             for step in range(1, blocks)
@@ -93,22 +177,22 @@
     ]
     own = [
         remote(
-            pan.at[p, :, :, pan_cols(block)], tau.at[p, :, tau_rows(space), :],
+            pan.at[p, :, :, pan_cols(block)], tau_rows(p, space),
             s_own.at[p], r_own.at[p], at(other_side),
         )
         for p in range(pairs)
     ]
     keep = [
         pltpu.make_async_copy(
-            pan.at[p, :, :, pan_cols(block)], tau.at[p, :, tau_rows(space), :], s_loc.at[p]
+            pan.at[p, :, :, pan_cols(block)], tau_rows(p, space), s_loc.at[p]
         )
         for p in range(pairs)
     ]
     forward = [
         [
             remote(
-                tau.at[p, :, tau_rows(sender(step) * 2 + side), :],
-                tau.at[p, :, tau_rows(sender(step) * 2 + side), :],
+                tau_rows(p, sender(step) * 2 + side),
+                tau_rows(p, sender(step) * 2 + side),
                 s_fwd.at[p, step - 1], r_fwd.at[p, step - 1], at(other_side),
             )
             for step in range(1, blocks)
@@ -116,39 +200,40 @@
         for p in range(pairs)
     ]
     my_half = pl.ds(pl.multiple_of(side * hrows, hrows), hrows)
-    far_half = pl.ds(pl.multiple_of((1 - side) * hrows, hrows), hrows)
-    my_piece = pl.ds(pl.multiple_of(side * hrows + block * prows, prows), prows)
-    halves = [
-        remote(part.at[m, far_half, :], got_half.at[m], s_half.at[m], r_half.at[m], at(other_side))
-        for m in range(moms)
-    ]
-    pieces = [
+    steps = []
+    size, base, landing, bit = vectors, 0, 0, 1
+    while bit < blocks:
+        own_bit = (block // bit) % 2
+        kinds = [(own_bit, (block + bit * (1 - 2 * own_bit)) * 2 + side)]
+        if bit == 1:
+            kinds.append((side, other_side))
+        for mine, partner in kinds:
+            size //= 2
+            near = pl.ds(pl.multiple_of(base + mine * size, size), size)
+            far = pl.ds(pl.multiple_of(base + (1 - mine) * size, size), size)
+            steps.append((partner, near, far, pl.ds(landing, size)))
+            base = base + mine * size
+            landing += size
+        bit *= 2
+    sums = [
         [
             remote(
-                half16.at[m, pl.ds(pl.multiple_of(peer(step) * prows, prows), prows), :],
-                got_piece.at[step - 1, m],
-                s_piece.at[m, step - 1], r_piece.at[m, step - 1], at(peer(step) * 2 + side),
+                part.at[m, far, :], got.at[m, land, :],
+                s_sum.at[k, m], r_sum.at[k, m], at(partner),
             )
-            for step in range(1, blocks)
+            for m in range(moms)
         ]
-        for m in range(moms)
+        for k, (partner, near, far, land) in enumerate(steps)
     ]
     fields = [
         [
             remote(
-                mes.at[core, m, my_piece, :], mes.at[core, m, my_piece, :],
-                s_field.at[m, step - 1], r_field.at[m, step - 1], at(peer(step) * 2 + side),
+                mes.at[core, m, near, :], mes.at[core, m, near, :],
+                s_field.at[k, m], r_field.at[k, m], at(partner),
             )
-            for step in range(1, blocks)
+            for m in range(moms)
         ]
-        for m in range(moms)
-    ]
-    swaps = [
-        remote(
-            mes.at[core, m, my_half, :], mes.at[core, m, my_half, :],
-            s_swap.at[m], r_swap.at[m], at(other_side),
-        )
-        for m in range(moms)
+        for k, (partner, near, far, land) in enumerate(steps)
     ]
     cores = [
         [
@@ -156,7 +241,7 @@
                 mes.at[core, m, which, :], mes.at[core, m, which, :],
                 s_core.at[m, i], r_core.at[m, i], {"tm": 1 - core},
             )
-            for i, which in enumerate((my_half, far_half))
+            for i, which in enumerate(steps[0][1:3])
         ]
         for m in range(moms)
     ]
@@ -170,51 +255,13 @@
             along[p][step].wait_recv()
             forward[p][step].start()
 
-    put = [pltpu.make_async_copy(made.at[p], out.at[p], s_out.at[p]) for p in range(pairs)]
-    turned = (((1,), (1,)), ((), ()))
+    put = [pltpu.make_async_copy(made.at[p], out.at[p], s_out.at[p]) for p in range(pairs - 1)]
 
     def dress(p):
-        from_first = pair_list[0, p] == 0
-        to_first = pair_list[1, p] == 0
-        for m in range(moms):
-            field = jnp.where(from_first, mes[0, m, my_half, :], mes[1, m, my_half, :])
-            real_part = field[:, :vectors]
-            imag_part = field[:, vectors:]
-            left[pl.ds(2 * m * hrows, hrows), :vectors] = real_part
-            left[pl.ds(2 * m * hrows, hrows), vectors:] = imag_part
-            left[pl.ds((2 * m + 1) * hrows, hrows), :vectors] = -imag_part
-            left[pl.ds((2 * m + 1) * hrows, hrows), vectors:] = real_part
-        for spin in range(blocks):
-            spin_rows = pl.ds(spin * vectors, vectors)
-            value = lax.dot_general(
-                left[:, :vectors], tau[p, 0, spin_rows, :], turned,
-                preferred_element_type=jnp.float32,
-            ) + lax.dot_general(
-                left[:, vectors:], tau[p, 1, spin_rows, :], turned,
-                preferred_element_type=jnp.float32,
-            )
-            value = value.astype(jnp.bfloat16)
-            for m in range(moms):
-                for o in range(2):
-                    right[m, pl.ds(spin * hrows, hrows), o * vectors : (o + 1) * vectors] = value[
-                        (2 * m + o) * hrows : (2 * m + o + 1) * hrows
-                    ]
-        for m in range(moms):
-            field = jnp.where(to_first, mes[0, m], mes[1, m])
-            real_part = field[:, :vectors]
-            imag_part = field[:, vectors:]
-            sink[:vectors, :vectors] = real_part
-            sink[:vectors, vectors:] = -imag_part
-            sink[vectors:, :vectors] = imag_part
-            sink[vectors:, vectors:] = real_part
-            value = lax.dot_general(
-                right[m], sink[...], turned, preferred_element_type=jnp.float32
-            ).astype(jnp.bfloat16)
-            for spin in range(blocks):
-                for o in range(2):
-                    made[p, m, o, :, pl.ds(spin * vectors, vectors)] = value[
-                        spin * hrows : (spin + 1) * hrows, o * vectors : (o + 1) * vectors
-                    ]
+        products(
+            pair_list[0, p] == 0, pair_list[1, p] == 0, my_half, tau.at[p], mes, made.at[p],
+            left, right, sink,
+        )
         put[p].start()
 
     def settle(p):
@@ -223,8 +270,7 @@
         for copy in forward[p]:
             copy.wait_recv()
 
-    for p in range(min(2, pairs)):
-        send_along(p)
+    send_along(0)
     own[0].start()
     for copy in keep:
         copy.start()
@@ -266,64 +312,73 @@
         )
         gram[m] = total
         part[m] = total.astype(jnp.bfloat16)
-        halves[m].start()
-
+        sums[0][m].start()
+
+    def add_up(k):
+        _, near, _, land = steps[k]
+        for m in range(moms):
+            sums[k][m].wait_recv()
+            value = gram[m, near, :] + got[m, land, :].astype(jnp.float32)
+            if k + 1 < len(steps):
+                gram[m, near, :] = value
+                part[m, near, :] = value.astype(jnp.bfloat16)
+                sums[k + 1][m].start()
+            else:
+                mes[core, m, near, :] = value.astype(jnp.bfloat16)
+                fields[k][m].start()
+
+    send_along(1)
+    add_up(0)
     for p in range(1, pairs):
         own[p].start()
-    for m in range(moms):
-        halves[m].wait_recv()
-        value = gram[m, my_half, :] + got_half[m].astype(jnp.float32)
-        half32[m] = value
-        half16[m] = value.astype(jnp.bfloat16)
-        for copy in pieces[m]:
-            copy.start()
-    for p in range(2, min(3, pairs)):
-        send_along(p)
     pass_on(0)
-
-    for m in range(moms):
-        value = half32[m, pl.ds(pl.multiple_of(block * prows, prows), prows), :]
-        for step in range(blocks - 1):
-            pieces[m][step].wait_recv()
-            value = value + got_piece[step, m].astype(jnp.float32)
-        mes[core, m, my_piece, :] = value.astype(jnp.bfloat16)
-        for copy in fields[m]:
-            copy.start()
+    for k in range(1, len(steps)):
+        add_up(k)
+    send_along(2)
+    pass_on(1)
+    for k in reversed(range(1, len(steps))):
+        for m in range(moms):
+            fields[k][m].wait_recv()
+            fields[k - 1][m].start()
+            if k == 1:
+                cores[m][0].start()
     for p in range(3, pairs):
         send_along(p)
-    if pairs > 1:
-        pass_on(1)
-    for m in range(moms):
-        for copy in fields[m]:
-            copy.wait_recv()
-        swaps[m].start()
-        cores[m][0].start()
-    if pairs > 2:
-        pass_on(2)
-    for m in range(moms):
-        swaps[m].wait_recv()
+    for p in range(2, pairs - 1):
+        pass_on(p)
+    for m in range(moms):
+        fields[0][m].wait_recv()
         cores[m][1].start()
     for m in range(moms):
         for copy in cores[m]:
             copy.wait_recv()
-    settle(0)
-    dress(0)
-    for p in range(3, pairs):
-        pass_on(p)
-    for p in range(1, pairs):
+    keep_mes = pltpu.make_async_copy(mes, mes_out, s_mes)
+    keep_mes.start()
+    last = pairs - 1
+    for p in range(last):
         settle(p)
         dress(p)
-
-    for m in range(moms):
-        halves[m].wait_send()
-        swaps[m].wait_send()
-        for copy in pieces[m] + fields[m] + cores[m]:
+        if p < blocks - 1:
+            along[last][p].wait_recv()
+            forward[last][p].start()
+    for step in range(last, blocks - 1):
+        along[last][step].wait_recv()
+        forward[last][step].start()
+    settle(last)
+
+    for m in range(moms):
+        for k in range(len(steps)):
+            sums[k][m].wait_send()
+            fields[k][m].wait_send()
+        for copy in cores[m]:
             copy.wait_send()
     for p in range(pairs):
         own[p].wait_send()
         for copy in along[p] + forward[p]:
             copy.wait_send()
-        put[p].wait()
+    for copy in put:
+        copy.wait()
+    keep_mes.wait()
 
 
 def exchange(eigvecs, momenta, pair_list, panels, spins):
@@ -334,47 +389,48 @@
     slices = lax.axis_size("tm")
     factor = 1.0 / math.sqrt(6.0 * sites * space_count * vectors)
     hrows = vectors // 2
-    prows = hrows // spins
+    steps = spins.bit_length()
     bf16, f32 = jnp.bfloat16, jnp.float32
     dma = pltpu.SemaphoreType.DMA
     others = spins - 1
     smem = pl.BlockSpec(memory_space=pltpu.SMEM)
-    hbm = pl.BlockSpec(memory_space=pl.ANY)
+    hbm = pl.BlockSpec(memory_space=pltpu.HBM)
+    anywhere = pl.BlockSpec(memory_space=pl.ANY)
     return pl.pallas_call(
         functools.partial(exchange_kernel, factor, spins),
-        out_shape=jax.ShapeDtypeStruct((pairs, moms, 2, rows, width), bf16),
+        out_shape=(
+            jax.ShapeDtypeStruct((pairs - 1, moms, 2, rows, width), bf16),
+            jax.ShapeDtypeStruct((2, rows * space_count, vectors), bf16),
+            jax.ShapeDtypeStruct((slices, moms, vectors, 2 * vectors), bf16),
+        ),
         in_specs=[smem, smem, hbm, hbm],
-        out_specs=hbm,
+        out_specs=(anywhere,) * 3,
         scratch_shapes=[
-            pltpu.VMEM((pairs, 2, rows * space_count, vectors), bf16),
+            pltpu.VMEM((pairs - 1, 2, rows * space_count, vectors), bf16),
             pltpu.VMEM((slices, moms, vectors, 2 * vectors), bf16),
             pltpu.VMEM((2 * moms * hrows, 2 * vectors), bf16),
             pltpu.VMEM((moms, spins * hrows, 2 * vectors), bf16),
             pltpu.VMEM((2 * vectors, 2 * vectors), bf16),
-            pltpu.VMEM((pairs, moms, 2, rows, width), bf16),
+            pltpu.VMEM((pairs - 1, moms, 2, rows, width), bf16),
             pltpu.VMEM((2, colors, sites, vectors), bf16),
             pltpu.VMEM((2 * colors * sites, vectors), bf16),
             pltpu.VMEM((2 * colors * sites, 2 * vectors), bf16),
             pltpu.VMEM((moms, vectors, 2 * vectors), f32),
             pltpu.VMEM((moms, vectors, 2 * vectors), bf16),
-            pltpu.VMEM((moms, hrows, 2 * vectors), bf16),
-            pltpu.VMEM((moms, hrows, 2 * vectors), f32),
-            pltpu.VMEM((moms, hrows, 2 * vectors), bf16),
-            pltpu.VMEM((others, moms, prows, 2 * vectors), bf16),
-            dma((moms,)), dma((moms,)),
-            dma((moms, others)), dma((moms, others)),
-            dma((moms, others)), dma((moms, others)),
-            dma((moms,)), dma((moms,)),
+            pltpu.VMEM((moms, vectors, 2 * vectors), bf16),
+            dma((steps, moms)), dma((steps, moms)),
+            dma((steps, moms)), dma((steps, moms)),
             dma((moms, 2)), dma((moms, 2)),
             dma((pairs, others)), dma((pairs, others)),
             dma((pairs,)), dma((pairs,)),
             dma((pairs, others)), dma((pairs, others)),
             dma((pairs,)),
             dma,
-            dma((pairs,)),
+            dma((pairs - 1,)),
+            dma,
         ],
         compiler_params=pltpu.CompilerParams(
-            collective_id=0, has_side_effects=True, vmem_limit_bytes=60 << 20
+            collective_id=0, has_side_effects=True, vmem_limit_bytes=36 << 20
         ),
         name="exchange",
     )(momenta, pair_list, eigvecs, panels)
@@ -382,7 +438,9 @@
 
 def local_kernels(eigvecs, momenta, pair_list, panels):
     spins = panels.shape[3] // eigvecs.shape[4]
-    return exchange(eigvecs, momenta, pair_list.T, panels, spins)
+    done, tau, mes = exchange(eigvecs, momenta, pair_list.T, panels, spins)
+    side = jnp.reshape(lax.axis_index("space") % 2, (1,)).astype(jnp.int32)
+    return finish(pair_list.T, side, done, tau, mes)
 
 
 def phased_block(cosine, sine_part, real_part, imag_part):
@@ -465,6 +523,7 @@
         and spins & (spins - 1) == 0
         and LX & (LX - 1) == 0
         and momenta.shape[0] <= 128
+        and pair_list.shape[0] > 2
         and panels.shape[2] * 2 == vectors
         and panels.shape[2] % 128 == 0
         and (vectors // 2) % (16 * spins) == 0

time: 98.3 us -> 91.2 us (0.928)
  the two profiles are of different devices: /device:TPU:0 before, /device:TPU:11 now
where the time goes in v3:
time: 91.2 us; the launch traced here: 91 us
  Pallas kernels  86.9 us (95%)
  local copies, waits for them, and re-layouts  4.01 us (4%)
    pallas_call x1, Pallas kernels, exchange(): pl.pallas_call(functools.partial(exchange_kernel, factor, spins), out_sha...  83.4 us
    unnamed x8, local copies, waits for them, and re-layouts  4.01 us
    pallas_call x1, Pallas kernels, finish(): pl.pallas_call(finish_kernel, out_shape=jax.ShapeDtypeStruct((last + 1,)...  3.55 us

profile of v3, /device:TPU:11, one launch (start us, length us, event | category | flops | bytes accessed | tf_op | source)
XLA Modules:
  0.0 91.0 jit_solution(9446458460758710922)
XLA Ops:
  0.0 0.0 copy-start
  0.0 1.6 %copy-done = bf16[4,2,128,1024]{3,2,1,0:T(8,128)(2,1)S(1)} copy-done((bf16[4,2,128,1024]{3,2,1,0:T(8,128)(2,1)S(1)}, bf16[4,2,128,1024]{3,2,1,0:T(8,128)(2,1)}, u32[]{:S(2)}) %copy-start) | copy-done | bytes 2097176
  1.6 0.0 copy-start.1
  1.6 1.1 %copy-done.1 = bf16[1,2,3,192,256]{4,3,2,1,0:T(8,128)(2,1)S(1)} copy-done((bf16[1,2,3,192,256]{4,3,2,1,0:T(8,128)(2,1)S(1)}, bf16[1,2,3,192,256]{4,3,2,1,0:T(8,128)(2,1)}, u32[]{:S(2)}) %copy-start.1) | copy-done | bytes 589848
  2.7 0.0 copy-start.2
  2.7 0.7 copy-done.2
  3.3 0.0 copy-start.3
  3.3 0.7 copy-done.3
  4.0 83.4 %exchange.1 = (bf16[3,3,2,128,1024]{4,3,2,1,0:T(8,128)(2,1)S(1)}, bf16[2,1024,256]{2,1,0:T(8,128)(2,1)S(1)}, bf16[2,3,256,512]{3,2,1,0:T(8,128)(2,1)S(1)}) custom-call(s32[3,3]{1,0:T(4,128)S(1)} %copy-done.3, s32[2,4]{1,0:T(2,128)S(1)} %bitcast.2, bf16[1,2,3,192,256]{4,3,2,1,0:T(8,128)(2,1)S(1)} %copy-done.1, bf16[4,2,128,1024]{3,2,1,0:T(8,128)(2,1)S(1)} %copy-done), custom_call_target="tpu_custom_call" | custom-call | tf_op jit(solution)/shard_map/exchange/pallas_call | solution.py:399
  87.4 3.5 %finish.1 = bf16[4,3,2,128,1024]{4,3,2,1,0:T(8,128)(2,1)} custom-call(s32[2,4]{1,0:T(2,128)S(1)} %bitcast.3, s32[1]{0:T(128)} %bitcast.1.side, bf16[3,3,2,128,1024]{4,3,2,1,0:T(8,128)(2,1)S(1)} %get-tuple-element.8.done, bf16[2,1024,256]{2,1,0:T(8,128)(2,1)S(1)} %get-tuple-element.9.tau, bf16[2,3,256,512]{3,2,1,0:T(8,128)(2,1)S(1)} %get-tuple-element.10.mes), custom_call_target="tpu_custom_call" | custom-call | tf_op jit(solution)/shard_map/finish/pallas_call | solution.py:96
Async XLA Ops:
  0.0 1.6 %copy-start = (bf16[4,2,128,1024]{3,2,1,0:T(8,128)(2,1)S(1)}, bf16[4,2,128,1024]{3,2,1,0:T(8,128)(2,1)}, u32[]{:S(2)}) copy-start(bf16[4,2,128,1024]{3,2,1,0:T(8,128)(2,1)} %pan.1) | copy-start | bytes 6291460
  1.6 1.1 %copy-start.1 = (bf16[1,2,3,192,256]{4,3,2,1,0:T(8,128)(2,1)S(1)}, bf16[1,2,3,192,256]{4,3,2,1,0:T(8,128)(2,1)}, u32[]{:S(2)}) copy-start(bf16[1,2,3,192,256]{4,3,2,1,0:T(8,128)(2,1)} %eig_hbm.1) | copy-start | bytes 1769476
  2.7 0.7 copy-start.2
  3.3 0.7 copy-start.3

commit v4 on v3

--- a/solution.py
+++ b/solution.py
@@ -271,7 +271,8 @@
             copy.wait_recv()
 
     send_along(0)
-    own[0].start()
+    for copy in own:
+        copy.start()
     for copy in keep:
         copy.start()
 
@@ -329,8 +330,6 @@
 
     send_along(1)
     add_up(0)
-    for p in range(1, pairs):
-        own[p].start()
     pass_on(0)
     for k in range(1, len(steps)):
         add_up(k)

time: 91.2 us -> 84.8 us (0.930)
  the two profiles are of different devices: /device:TPU:11 before, /device:TPU:0 now
where the time goes in v4:
time: 84.8 us; the launch traced here: 84.5 us
  Pallas kernels  80.5 us (95%)
  local copies, waits for them, and re-layouts  4.01 us (5%)
    pallas_call x1, Pallas kernels, exchange(): pl.pallas_call(functools.partial(exchange_kernel, factor, spins), out_sha...  77 us
    unnamed x8, local copies, waits for them, and re-layouts  4.01 us
    pallas_call x1, Pallas kernels, finish(): pl.pallas_call(finish_kernel, out_shape=jax.ShapeDtypeStruct((last + 1,)...  3.55 us

profile of v4, /device:TPU:0, one launch (start us, length us, event | category | flops | bytes accessed | tf_op | source)
XLA Modules:
  0.0 84.5 jit_solution(13401007467367221685)
XLA Ops:
  0.0 0.0 copy-start
  0.0 1.6 %copy-done = bf16[4,2,128,1024]{3,2,1,0:T(8,128)(2,1)S(1)} copy-done((bf16[4,2,128,1024]{3,2,1,0:T(8,128)(2,1)S(1)}, bf16[4,2,128,1024]{3,2,1,0:T(8,128)(2,1)}, u32[]{:S(2)}) %copy-start) | copy-done | bytes 2097176
  1.6 0.0 copy-start.1
  1.6 1.1 %copy-done.1 = bf16[1,2,3,192,256]{4,3,2,1,0:T(8,128)(2,1)S(1)} copy-done((bf16[1,2,3,192,256]{4,3,2,1,0:T(8,128)(2,1)S(1)}, bf16[1,2,3,192,256]{4,3,2,1,0:T(8,128)(2,1)}, u32[]{:S(2)}) %copy-start.1) | copy-done | bytes 589848
  2.7 0.0 copy-start.2
  2.7 0.7 copy-done.2
  3.3 0.0 copy-start.3
  3.3 0.7 copy-done.3
  4.0 77.0 %exchange.1 = (bf16[3,3,2,128,1024]{4,3,2,1,0:T(8,128)(2,1)S(1)}, bf16[2,1024,256]{2,1,0:T(8,128)(2,1)S(1)}, bf16[2,3,256,512]{3,2,1,0:T(8,128)(2,1)S(1)}) custom-call(s32[3,3]{1,0:T(4,128)S(1)} %copy-done.3, s32[2,4]{1,0:T(2,128)S(1)} %bitcast.2, bf16[1,2,3,192,256]{4,3,2,1,0:T(8,128)(2,1)S(1)} %copy-done.1, bf16[4,2,128,1024]{3,2,1,0:T(8,128)(2,1)S(1)} %copy-done), custom_call_target="tpu_custom_call" | custom-call | tf_op jit(solution)/shard_map/exchange/pallas_call | solution.py:398
  81.0 3.5 %finish.1 = bf16[4,3,2,128,1024]{4,3,2,1,0:T(8,128)(2,1)} custom-call(s32[2,4]{1,0:T(2,128)S(1)} %bitcast.3, s32[1]{0:T(128)} %bitcast.1.side, bf16[3,3,2,128,1024]{4,3,2,1,0:T(8,128)(2,1)S(1)} %get-tuple-element.8.done, bf16[2,1024,256]{2,1,0:T(8,128)(2,1)S(1)} %get-tuple-element.9.tau, bf16[2,3,256,512]{3,2,1,0:T(8,128)(2,1)S(1)} %get-tuple-element.10.mes), custom_call_target="tpu_custom_call" | custom-call | tf_op jit(solution)/shard_map/finish/pallas_call | solution.py:96
Async XLA Ops:
  0.0 1.6 %copy-start = (bf16[4,2,128,1024]{3,2,1,0:T(8,128)(2,1)S(1)}, bf16[4,2,128,1024]{3,2,1,0:T(8,128)(2,1)}, u32[]{:S(2)}) copy-start(bf16[4,2,128,1024]{3,2,1,0:T(8,128)(2,1)} %pan.1) | copy-start | bytes 6291460
  1.6 1.1 %copy-start.1 = (bf16[1,2,3,192,256]{4,3,2,1,0:T(8,128)(2,1)S(1)}, bf16[1,2,3,192,256]{4,3,2,1,0:T(8,128)(2,1)}, u32[]{:S(2)}) copy-start(bf16[1,2,3,192,256]{4,3,2,1,0:T(8,128)(2,1)} %eig_hbm.1) | copy-start | bytes 1769476
  2.7 0.7 copy-start.2
  3.3 0.7 copy-start.3
